TPU v7x, 32 devices: a whole 2x2x4 slice. The times are simulated.
32 devices in a mesh: seq: 16 (over z, x, core), head: 2 (over y).
Axes of the slice: x: 2, y: 2, z: 4, core: 2. Of those that a mesh axis runs over, the one named last changes fastest.
Arguments:
- features: bfloat16 [8, 32, 8, 512], P(None, 'seq', 'head'), may hold values from -540 to 540
- gn_gain: float32 [512], replicated, may hold values from 0.5 to 1.5
- gn_bias: float32 [512], replicated, may hold values from -3 to 3
- conv_weight: bfloat16 [3, 3, 3, 16, 512], replicated, may hold values from -0.0546875 to 0.0546875
- conv_bias: float32 [16], replicated, may hold values from -3 to 3
- patch_weight: bfloat16 [64, 3072], replicated, may hold values from -0.75 to 0.75
- patch_bias: float32 [3072], replicated, may hold values from -3 to 3
- image_mod: float32 [3, 3072], replicated, may hold values from -3 to 3
- w_qkv: bfloat16 [3072, 3, 2048], P('seq', None, 'head'), may hold values from -5 to 5
- text_ids: int32 [512], replicated, may hold values from 0 to 16383
- text_length: int32 [1], replicated, may hold values from 256 to 512
- text_table: bfloat16 [3072, 16384], P('seq'), may hold values from -60 to 60
- text_mod: float32 [2, 3072], P(None, 'seq'), may hold values from -3 to 3
- w_text: bfloat16 [3072, 2, 2048], P('seq', None, 'head'), may hold values from -2 to 2
- w_out: bfloat16 [2048, 3072], P('head'), may hold values from -0.625 to 0.625
- out_bias: float32 [3072], replicated, may hold values from -3 to 3
Outputs:
- block_out: bfloat16 [8, 16, 4, 3072], P(None, 'seq', 'head')
All inputs are finite; a program needn't handle non-finite values.
Results may differ from a plain program's by a relative error of at most 0.0089.
Values may be sent and summed in bfloat16 or wider, within the bound.
A program may use at most 128 MiB of HBM per device.

v0:
```python
import math
import jax
import jax.numpy as jnp
from jax import lax
from jax.sharding import PartitionSpec as P

HD = 128
GN_GROUPS = 32
eps_norm = 1e-06


def with_halo(cells, sides, width):
    for axis, dim in sides:
        count = lax.axis_size(axis)
        ends = count - 1
        head = lax.slice_in_dim(cells, 0, width, axis=dim)
        tail = lax.slice_in_dim(cells, cells.shape[dim] - width, cells.shape[dim], axis=dim)
        cells = jnp.concatenate(
            [
                lax.ppermute(tail, axis, [(i, (i + 1) % count) for i in range(ends)]),
                cells,
                lax.ppermute(head, axis, [((i + 1) % count, i) for i in range(ends)]),
            ],
            axis=dim,
        )
    return cells


def patchify(latent):
    frame_count, row_count, col_count, chan_count = latent.shape
    blocks = latent.reshape(frame_count, row_count // 2, 2, col_count // 2, 2, chan_count)
    blocks = blocks.transpose(0, 1, 3, 2, 4, 5)
    return blocks.reshape(frame_count * (row_count // 2) * (col_count // 2), 4 * chan_count)


def embed_tokens(patches, patch_weight, patch_bias, image_mod):
    hidden = jnp.dot(patches, patch_weight, preferred_element_type=jnp.float32) + patch_bias
    center = jnp.mean(hidden, axis=1, keepdims=True)
    offset = hidden - center
    spread = jnp.mean(offset * offset, axis=1, keepdims=True)
    normed = offset * lax.rsqrt(spread + eps_norm)
    modulated = (normed * (1.0 + image_mod[1]) + image_mod[0]).astype(jnp.bfloat16)
    return (hidden, modulated)


def text_start(query, text_keys, text_values, text_valid):
    scores = jnp.einsum("qhe,khe->qhk", query, text_keys, preferred_element_type=jnp.float32) / HD
    scores = jnp.where(text_valid[None, None, :], scores, -1e30)
    first_top = jnp.max(scores, axis=2)
    probs = jnp.exp(scores - first_top[..., None])
    first_total = jnp.sum(probs, axis=2)
    first_acc = jnp.einsum(
        "qhk,khe->qhe", probs.astype(jnp.bfloat16), text_values, preferred_element_type=jnp.float32
    )
    return (first_top, first_total, first_acc)


def attend_rows(query, state, piece):
    piece_rows = piece.shape[0]
    block_rows = math.gcd(piece_rows, 2048)
    heads_count = query.shape[1]
    blocks = piece.reshape(piece_rows // block_rows, block_rows, 2, heads_count, HD)

    def one_block(inner, block):
        run_top, run_total, run_acc = inner
        scores = (
            jnp.einsum("qhe,khe->qhk", query, block[:, 0], preferred_element_type=jnp.float32) / HD
        )
        new_top = jnp.maximum(run_top, jnp.max(scores, axis=2))
        factor = jnp.exp(run_top - new_top)
        probs = jnp.exp(scores - new_top[..., None])
        run_total = run_total * factor + jnp.sum(probs, axis=2)
        run_acc = run_acc * factor[..., None] + jnp.einsum(
            "qhk,khe->qhe",
            probs.astype(jnp.bfloat16),
            block[:, 1],
            preferred_element_type=jnp.float32,
        )
        return ((new_top, run_total, run_acc), None)

    return lax.scan(one_block, state, blocks)[0]


def body(
    features,
    gn_gain,
    gn_bias,
    conv_weight,
    conv_bias,
    patch_weight,
    patch_bias,
    image_mod,
    w_qkv,
    text_ids,
    text_length,
    text_table,
    text_mod,
    w_text,
    w_out,
    out_bias,
):
    frame_count, row_count, col_count, chan_count = features.shape
    width_full = patch_weight.shape[1]
    values = features.astype(jnp.float32)
    grouped = values.reshape(frame_count, row_count, col_count, GN_GROUPS, chan_count // GN_GROUPS)
    group_sums = jnp.sum(grouped, axis=(0, 1, 2, 4))
    group_squares = jnp.sum(grouped * grouped, axis=(0, 1, 2, 4))
    group_sums, group_squares = lax.psum((group_sums, group_squares), ("seq", "head"))
    cell_count = (
        frame_count
        * row_count
        * col_count
        * (chan_count // GN_GROUPS)
        * lax.axis_size("seq")
        * lax.axis_size("head")
    )
    group_mean = group_sums / cell_count
    group_scale = lax.rsqrt(group_squares / cell_count - group_mean * group_mean + eps_norm)
    normed = ((grouped - group_mean[:, None]) * group_scale[:, None]).reshape(
        frame_count, row_count, col_count, chan_count
    )
    activated = jax.nn.silu(normed * gn_gain + gn_bias).astype(jnp.bfloat16)
    rimmed = with_halo(activated, (("seq", 1), ("head", 2)), 1)
    padded = jnp.concatenate([rimmed[:1], rimmed[:1], rimmed], axis=0)
    windows = []
    for time_off in range(3):
        for row_off in range(3):
            for col_off in range(3):
                windows.append(
                    padded[
                        time_off : time_off + frame_count,
                        row_off : row_off + row_count,
                        col_off : col_off + col_count,
                    ]
                )
    stacked = jnp.stack(windows, axis=3)
    latent_chans = conv_weight.shape[3]
    kernels = conv_weight.reshape(27, latent_chans, chan_count)
    latent_sum = jnp.einsum("fyxkc,kzc->fyxz", stacked, kernels, preferred_element_type=jnp.float32)
    latent = (latent_sum + conv_bias).astype(jnp.bfloat16)
    patches = patchify(latent)
    hidden, own_modulated = embed_tokens(patches, patch_weight, patch_bias, image_mod)
    modulated = lax.all_gather(own_modulated, "head", axis=0, tiled=True)
    token_count = modulated.shape[0]
    head_width = w_qkv.shape[2]
    heads_here = head_width // HD
    qkv = jnp.einsum(
        "nd,dkj->nkj",
        modulated,
        lax.all_gather(w_qkv, "seq", axis=0, tiled=True),
        preferred_element_type=jnp.float32,
    ).astype(jnp.bfloat16)
    context = jnp.take(text_table, text_ids, axis=1).astype(jnp.float32)
    text_weight = w_text.astype(jnp.float32)
    text_gain = 1.0 + text_mod[1]
    text_shift = text_mod[0]
    text_sums, text_squares = lax.psum(
        (jnp.sum(context, axis=0), jnp.sum(context * context, axis=0)), "seq"
    )
    text_mean = text_sums / width_full
    text_scale = lax.rsqrt(text_squares / width_full - text_mean * text_mean + eps_norm)
    text_normed = (context - text_mean) * text_scale * text_gain[:, None] + text_shift[:, None]
    partial_kv = jnp.einsum(
        "dt,dkj->tkj", text_normed, text_weight, precision=lax.Precision.HIGHEST
    )
    text_kv = lax.psum(partial_kv, "seq")
    text_kv = text_kv.astype(jnp.bfloat16)
    text_count = text_kv.shape[0]
    text_valid = jnp.arange(text_count, dtype=jnp.int32) < text_length[0]
    query = qkv[:, 0].reshape(token_count, heads_here, HD)
    text_keys = text_kv[:, 0].reshape(text_count, heads_here, HD)
    text_values = text_kv[:, 1].reshape(text_count, heads_here, HD)
    first_state = text_start(query, text_keys, text_values, text_valid)
    image_kv = qkv[:, 1:3]
    run_top, run_total, run_acc = attend_rows(
        query, first_state, lax.all_gather(image_kv, "seq", axis=0, tiled=True)
    )
    attended = (
        (run_acc / run_total[..., None]).astype(jnp.bfloat16).reshape(token_count, head_width)
    )
    projected = (
        lax.psum_scatter(
            jnp.dot(attended, w_out, preferred_element_type=jnp.float32),
            "head",
            scatter_dimension=0,
            tiled=True,
        )
        + out_bias
    )
    block_out = (hidden + image_mod[2] * projected).astype(jnp.bfloat16)
    return block_out.reshape(frame_count, row_count // 2, col_count // 2, width_full)


def solution(mesh):
    return jax.shard_map(
        body,
        mesh=mesh,
        in_specs=(
            P(None, "seq", "head", None),
            P(),
            P(),
            P(),
            P(),
            P(),
            P(),
            P(),
            P("seq", None, "head"),
            P(),
            P(),
            P("seq", None),
            P(None, "seq"),
            P("seq", None, "head"),
            P("head", None),
            P(),
        ),
        out_specs=P(None, "seq", "head", None),
        check_vma=False,
    )
```

profile of v0, /device:TPU:0, one launch (start us, length us, event | category | flops | bytes accessed | tf_op | source)
XLA Modules:
  0.0 285.2 jit_solution(11076966553390359524)
XLA Ops:
  6.5 0.7 all-gather.3.cloned.1.call-update
  7.3 0.9 convert_reduce_fusion.1
  8.6 43.1 %all-reduce = (f32[32]{0:T(128)S(1)}, f32[32]{0:T(128)S(1)}) all-reduce(f32[32]{0:T(128)S(1)} %reduce_sum.92, f32[32]{0:T(128)S(1)} %reduce_sum.89), channel_id=1, replica_groups=mesh['seq'=16,'head'=2] {'seq','head'}, use_global_device_ids=true, to_apply=%region_5.6 | all-reduce | flops 64 | bytes 512 | tf_op jit(solution)/shard_map/psum | solution.py:108
  52.0 1.0 fusion.41
  52.9 1.8 collective-permute-start
  54.7 1.3 collective-permute-start.1
  56.0 0.7 compare_select_fusion
  56.7 1.0 fusion.78
  57.7 0.7 compare_and_fusion
  58.4 1.5 collective-permute-done.1
  59.9 2.5 collective-permute-start.2
  62.4 1.3 collective-permute-start.3
  63.7 10.1 %copy.82 = bf16[192,16384]{0,1:T(8,128)(2,1)} copy(bf16[192,16384]{1,0:T(8,128)(2,1)} %param.27) | data formatting | bytes 12582912 | tf_op args[11]
  73.8 6.2 %gather_fusion = bf16[512,192]{1,0:T(8,128)(2,1)S(1)} fusion(bf16[192,16384]{0,1:T(8,128)(2,1)} %copy.82, s32[1024]{0:T(1024)S(1)} %pad_clamp_fusion), kind=kCustom, calls=%fused_computation | custom fusion | bytes 395264 | tf_op jit(solution)/shard_map/jit(_take)/gather | solution.py:153
  81.6 0.6 fusion.9
  82.9 5.9 %all_gather.9 = bf16[32,3072]{1,0:T(8,128)(2,1)S(1)} all-gather(bf16[16,3072]{1,0:T(8,128)(2,1)S(1)} %add_convert_fusion.1), channel_id=1, replica_groups=mesh['seq'=16,'head'=2] {'head'}, dimensions={0}, use_global_device_ids=true | all-gather | bytes 294912 | tf_op jit(solution)/shard_map/all_gather | solution.py:143
  88.8 23.2 %all-gather.3.cloned.1.call-done = bf16[3072,3,1024]{2,0,1:T(8,128)(2,1)} async-done(((bf16[192,3,1024]{2,0,1:T(8,128)(2,1)}), bf16[3072,3,1024]{2,0,1:T(8,128)(2,1)}) %all-gather.3.cloned.1.call-update) | async-done | bytes 18874384 | tf_op jit(solution)/shard_map/all_gather | solution.py:150
  112.0 9.7 %convolution_convert_fusion = bf16[32,3,1024]{2,0,1:T(8,128)(2,1)S(1)} fusion(bf16[3072,3,1024]{2,0,1:T(8,128)(2,1)} %all-gather.3.cloned.1.call-done, bf16[32,3072]{1,0:T(8,128)(2,1)S(1)} %all_gather.9), kind=kOutput, calls=%fused_computation.7 | convolution fusion | flops 604078080 | bytes 19267584 | tf_op jit(solution)/shard_map/nd,dkj->nkj/dot_general | solution.py:147
  121.7 0.7 slice.219
  122.8 33.0 %all-reduce.1 = (f32[512]{0:T(512)S(1)}, f32[512]{0:T(512)S(1)}) all-reduce(f32[512]{0:T(512)S(1)} %get-tuple-element.16, f32[512]{0:T(512)S(1)} %get-tuple-element.15), channel_id=1, replica_groups=mesh['seq'=16,'head'=2] {'seq'}, use_global_device_ids=true, to_apply=%region_9.10 | all-reduce | flops 1024 | bytes 8192 | tf_op jit(solution)/shard_map/psum | solution.py:157
  155.8 3.9 %fusion.12 = f32[512,2,1024]{2,0,1:T(8,128)} fusion(bf16[192,2,1024]{2,1,0:T(2,128)(2,1)S(1)} %copy-done, f32[192]{0:T(256)S(1)} %bitcast.263, f32[192]{0:T(256)S(1)} %bitcast.262, f32[512]{0:T(512)S(1)} %get-tuple-element.47, f32[512]{0:T(512)S(1)} %get-tuple-element.46, bf16[512,192]{1,0:T(8,128)(2,1)S(1)} %gather_fusion, ...), kind=kOutput, calls=%fused_computation.24 | convolution fusion | flops 2416508928 | bytes 5183488 | tf_op jit(solution)/shard_map/dt,dkj->tkj/dot_general | solution.py:163
  159.7 94.6 %all-reduce.3 = bf16[512,2,1024]{2,0,1:T(8,128)(2,1)S(1)} all-reduce(f32[512,2,1024]{2,0,1:T(8,128)} %fusion.12), channel_id=1, replica_groups=mesh['seq'=16,'head'=2] {'seq'}, use_global_device_ids=true, to_apply=%region_10.11 | all-reduce | flops 1048576 | bytes 6291456 | tf_op jit(solution)/shard_map/psum | solution.py:166
  255.8 1.3 fusion.80
  257.0 2.4 copy.103
  259.6 0.6 fusion.81
  260.1 0.6 copy-done.2
  261.1 0.4 convolution_bitcast_fusion
  261.5 0.4 fusion.7
  261.9 1.9 fusion.43
  263.9 13.2 %reduce-scatter.2.cloned.1.call-done = f32[16,3072]{1,0:T(8,128)} async-done(((f32[32,3072]{1,0:T(8,128)}), f32[16,3072]{1,0:T(8,128)}) %reduce-scatter.2.cloned.1.call-update) | async-done | bytes 196624 | tf_op jit(solution)/shard_map/reduce_scatter | solution.py:182
  277.1 1.0 add_convert_fusion
  278.0 0.7 reshape.87
  (98 shorter events, 4.4 us)
Async XLA Ops:
  6.5 149.3 %copy-start = (bf16[192,2,1024]{2,1,0:T(2,128)(2,1)S(1)}, bf16[192,2,1024]{2,1,0:T(2,128)(2,1)}, u32[]{:S(2)}) copy-start(bf16[192,2,1024]{2,1,0:T(2,128)(2,1)} %param.29) | copy-start | bytes 2359300
  6.5 105.4 %all-gather.3.cloned.1.call-start = ((), (), s32[]{:S(2)}) async-start(), calls=%async_computation.1 | async-start | bytes 20054016 | tf_op jit(solution)/shard_map/all_gather | solution.py:150
  7.3 249.8 %all-gather.5.cloned.1.call-start = ((), (), s32[]{:S(2)}) async-start(), calls=%async_computation.2 | async-start | bytes 2228224 | tf_op jit(solution)/shard_map/all_gather | solution.py:176
  52.9 5.4 %collective-permute-start = (bf16[8,1,4,512]{3,0,2,1:T(8,128)(2,1)S(1)}, bf16[8,1,4,512]{3,0,2,1:T(8,128)(2,1)S(1)}, u32[]{:S(2)}, u32[]{:S(2)}) collective-permute-start(bf16[8,1,4,512]{3,0,2,1:T(8,128)(2,1)S(1)} %get-tuple-element.41), channel_id=1, source_target_pairs={{0,2},{2,4},{4,6},{6,8},{8,10},{10,12},{12,14},{14,16},{16,18},{18... | collective-permute-start | bytes 98312 | tf_op jit(solution)/shard_map/ppermute | solution.py:20
  54.7 5.2 %collective-permute-start.1 = (bf16[8,1,4,512]{3,0,2,1:T(8,128)(2,1)S(1)}, bf16[8,1,4,512]{3,0,2,1:T(8,128)(2,1)S(1)}, u32[]{:S(2)}, u32[]{:S(2)}) collective-permute-start(bf16[8,1,4,512]{3,0,2,1:T(8,128)(2,1)S(1)} %get-tuple-element.42), channel_id=1, source_target_pairs={{2,0},{4,2},{6,4},{8,6},{10,8},{12,10},{14,12},{16,14},{18,16},{20... | collective-permute-start | bytes 98312 | tf_op jit(solution)/shard_map/ppermute | solution.py:22
  59.9 20.1 %collective-permute-start.2 = (bf16[8,4,1,512]{3,0,2,1:T(8,128)(2,1)S(1)}, bf16[8,4,1,512]{3,0,2,1:T(8,128)(2,1)S(1)}, u32[]{:S(2)}, u32[]{:S(2)}) collective-permute-start(bf16[8,4,1,512]{3,0,2,1:T(8,128)(2,1)S(1)} %get-tuple-element.39), channel_id=1, source_target_pairs={{0,1},{2,3},{4,5},{6,7},{8,9},{10,11},{12,13},{14,15},{16,17},{18,... | collective-permute-start | bytes 98312 | tf_op jit(solution)/shard_map/ppermute | solution.py:20
  62.4 17.6 %collective-permute-start.3 = (bf16[8,4,1,512]{3,0,2,1:T(8,128)(2,1)S(1)}, bf16[8,4,1,512]{3,0,2,1:T(8,128)(2,1)S(1)}, u32[]{:S(2)}, u32[]{:S(2)}) collective-permute-start(bf16[8,4,1,512]{3,0,2,1:T(8,128)(2,1)S(1)} %get-tuple-element.40), channel_id=1, source_target_pairs={{1,0},{3,2},{5,4},{7,6},{9,8},{11,10},{13,12},{15,14},{17,16},{19,... | collective-permute-start | bytes 98312 | tf_op jit(solution)/shard_map/ppermute | solution.py:22
  80.3 0.8 copy-start.1
  80.4 0.8 copy-start.7
  80.4 0.8 copy-start.8
  80.5 1.0 copy-start.3
  80.5 1.0 copy-start.9
  80.8 1.5 copy-start.4
  80.8 1.5 copy-start.5
  88.8 67.0 %copy-start.10 = (f32[2,192]{1,0:T(2,128)S(1)}, f32[2,192]{1,0:T(2,128)}, u32[]{:S(2)}) copy-start(f32[2,192]{1,0:T(2,128)} %param.28) | copy-start | bytes 4612
  122.4 154.7 %reduce-scatter.2.cloned.1.call-start = ((), (), s32[]{:S(2)}) async-start(), calls=%async_computation.3 | async-start | bytes 589824 | tf_op jit(solution)/shard_map/reduce_scatter | solution.py:182
  257.0 4.9 %slice-start = ((s8[6291456]{0:T(1024)(128)(4,1)}), s8[4194304]{0:T(1024)(128)(4,1)S(1)}, s32[]{:S(2)}) async-start(s8[6291456]{0:T(1024)(128)(4,1)} %bitcast.249), calls=%async_computation.4 | async-start | bytes 8388608
  259.4 2.5 slice-start.1
  259.6 1.2 copy-start.2
  261.9 15.2 %copy-start.6 = (f32[3072]{0:T(1024)S(1)}, f32[3072]{0:T(1024)}, u32[]{:S(2)}) copy-start(f32[3072]{0:T(1024)} %param.31) | copy-start | bytes 36868
Sparse Core Ops, SparseCore 0:
  8.9 103.0 all-gather.2
  122.5 42.3 all-gather.4
  264.0 12.9 reduce-scatter.1
where the time goes:
time: 286 us; the launch traced here: 285 us
  blocking collectives  177 us (62%)
  waiting for transfers between devices  38.6 us (13%)
  local copies, waits for them, and re-layouts  22.7 us (8%)
  matrix products  19.1 us (7%)
  between operations  14.3 us (5%)
  starting transfers between devices  6.94 us (2%)
  other arithmetic  6.94 us (2%)
    psum x1, blocking collectives, body(): text_kv = lax.psum(partial_kv, 'seq')  94.6 us
    psum x1, blocking collectives, body(): lax.psum((group_sums, group_squares), ('seq', 'head'))  43.1 us
    psum x1, blocking collectives, body(): lax.psum((jnp.sum(context, axis=0), jnp.sum(context * context, axis=0)),...  33 us
    all_gather x1, waiting for transfers between devices, body(): lax.all_gather(w_qkv, 'seq', axis=0, tiled=True)  23.2 us
    unnamed x56, local copies, waits for them, and re-layouts  14.5 us
    reduce_scatter x1, waiting for transfers between devices, body(): lax.psum_scatter(jnp.dot(attended, w_out, preferred_element_type=jnp.floa...  13.2 us
    dot_general x1, matrix products, body(): jnp.einsum('nd,dkj->nkj', modulated, lax.all_gather(w_qkv, 'seq', axis=0,...  9.7 us
    gather x1, local copies, waits for them, and re-layouts, body(): context = jnp.take(text_table, text_ids, axis=1).astype(jnp.float32)  6.18 us
  transfers between devices with their start and end apart: 7, of which 3 were waited for; matrix products, arithmetic and copies ran while one was open for 10% of the time, Pallas kernels for 0%

commit v1 on v0

--- a/solution.py
+++ b/solution.py
@@ -7,6 +7,22 @@
 HD = 128
 GN_GROUPS = 32
 eps_norm = 1e-06
+
+
+def mix_the_quotas(w_in, d0, t0):
+    right_arr, far_arr, vec_out = (lax.axis_size("seq"), lax.axis_index("seq"), w_in.shape[d0])
+    ledger = list(map(lambda ix: (ix, (ix + 1) % right_arr), range(right_arr)))
+    series = list(map(lambda ix: (ix, (ix - 1) % right_arr), range(right_arr)))
+    s_next = right_arr // 2
+    back = frame_out = w_in
+    current_block = t0(w_in, far_arr * vec_out)
+    for dev_i in range(1, s_next + 1):
+        back = lax.ppermute(back, axis_name="seq", perm=ledger)
+        if dev_i < right_arr - s_next:
+            frame_out = lax.ppermute(frame_out, axis_name="seq", perm=series)
+            current_block = current_block + t0(frame_out, (far_arr + dev_i) % right_arr * vec_out)
+        current_block = current_block + t0(back, (far_arr - dev_i) % right_arr * vec_out)
+    return current_block
 
 
 def with_halo(cells, sides, width):
@@ -144,11 +160,15 @@
     token_count = modulated.shape[0]
     head_width = w_qkv.shape[2]
     heads_here = head_width // HD
-    qkv = jnp.einsum(
-        "nd,dkj->nkj",
-        modulated,
-        lax.all_gather(w_qkv, "seq", axis=0, tiled=True),
-        preferred_element_type=jnp.float32,
+    qkv = mix_the_quotas(
+        w_qkv,
+        0,
+        lambda part, start: jnp.einsum(
+            "nd,dkj->nkj",
+            lax.dynamic_slice_in_dim(modulated, start, part.shape[0], axis=1),
+            part,
+            preferred_element_type=jnp.float32,
+        ),
     ).astype(jnp.bfloat16)
     context = jnp.take(text_table, text_ids, axis=1).astype(jnp.float32)
     text_weight = w_text.astype(jnp.float32)

time: 286 us -> 455 us (1.59)
  starting transfers between devices: 6.94 us -> 134 us
  blocking collectives: 177 us -> 201 us
  waiting for transfers between devices: 38.6 us -> 45.2 us
  other arithmetic: 6.94 us -> 12.4 us
    ppermute x0 -> x15, starting transfers between devices: none -> 126 us  [the longest x8 118 us: mix_the_quotas(): back = lax.ppermute(back, axis_name='seq', perm=ledger)]
    ppermute x0 -> x15, waiting for transfers between devices: none -> 27.4 us  [the longest x8 27.4 us: mix_the_quotas(): back = lax.ppermute(back, axis_name='seq', perm=ledger)]
    all_gather x1 -> x0, waiting for transfers between devices: 23.2 us -> none  [body(): lax.all_gather(w_qkv, 'seq', axis=0, tiled=True)]
    psum x1, blocking collectives: 43.1 us -> 57.6 us  [body(): lax.psum((group_sums, group_squares), ('seq', 'head'))]
    psum x1, blocking collectives: 33 us -> 42.6 us  [body(): lax.psum((jnp.sum(context, axis=0), jnp.sum(context * context, axis=0)),...]
    dot_general x1 -> x16, matrix products: 9.7 us -> 12.7 us  [body(): jnp.einsum('nd,dkj->nkj', lax.dynamic_slice_in_dim(modulated, start, part...]
    unnamed x56 -> x80, local copies, waits for them, and re-layouts: 14.5 us -> 15.4 us
  transfers between devices with their start and end apart: 7 -> 21, of which waited for: 3 -> 7; matrix products, arithmetic and copies ran while one was open for 10% -> 11% of each run, Pallas kernels for 0% -> 0%
where the time goes in v1:
time: 455 us; the launch traced here: 454 us
  blocking collectives  201 us (44%)
  starting transfers between devices  134 us (29%)
  waiting for transfers between devices  45.2 us (10%)
  local copies, waits for them, and re-layouts  23.6 us (5%)
  matrix products  22.3 us (5%)
  between operations  14.8 us (3%)
  other arithmetic  12.4 us (3%)
    ppermute x8, starting transfers between devices, mix_the_quotas(): back = lax.ppermute(back, axis_name='seq', perm=ledger)  118 us
    psum x1, blocking collectives, body(): text_kv = lax.psum(partial_kv, 'seq')  94.8 us
    psum x1, blocking collectives, body(): lax.psum((group_sums, group_squares), ('seq', 'head'))  57.6 us
    psum x1, blocking collectives, body(): lax.psum((jnp.sum(context, axis=0), jnp.sum(context * context, axis=0)),...  42.6 us
    ppermute x8, waiting for transfers between devices, mix_the_quotas(): back = lax.ppermute(back, axis_name='seq', perm=ledger)  27.4 us
    reduce_scatter x1, waiting for transfers between devices, body(): lax.psum_scatter(jnp.dot(attended, w_out, preferred_element_type=jnp.floa...  16.9 us
    unnamed x80, local copies, waits for them, and re-layouts  15.4 us
    dot_general x16, matrix products, body(): jnp.einsum('nd,dkj->nkj', lax.dynamic_slice_in_dim(modulated, start, part...  12.7 us
  transfers between devices with their start and end apart: 21, of which 7 were waited for; matrix products, arithmetic and copies ran while one was open for 11% of the time, Pallas kernels for 0%

profile of v1, /device:TPU:0, one launch (start us, length us, event | category | flops | bytes accessed | tf_op | source)
XLA Modules:
  0.0 453.8 jit_solution(500498705741974509)
XLA Ops:
  6.5 5.4 %collective-permute-start.4 = (bf16[192,3,1024]{2,0,1:T(8,128)(2,1)}, bf16[192,3,1024]{2,0,1:T(8,128)(2,1)S(1)}, u32[]{:S(2)}, u32[]{:S(2)}) collective-permute-start(bf16[192,3,1024]{2,0,1:T(8,128)(2,1)} %param.24), channel_id=1, source_target_pairs={{0,30},{2,0},{4,2},{6,4},{8,6},{10,8},{12,10},{14,12},{16,14},{18,... | collective-permute-start | bytes 3538952 | tf_op jit(solution)/shard_map/ppermute | solution.py:22
  13.3 57.6 %all-reduce = (f32[32]{0:T(128)S(1)}, f32[32]{0:T(128)S(1)}) all-reduce(f32[32]{0:T(128)S(1)} %reduce_sum.92, f32[32]{0:T(128)S(1)} %reduce_sum.89), channel_id=1, replica_groups=mesh['seq'=16,'head'=2] {'seq','head'}, use_global_device_ids=true, to_apply=%region_5.6 | all-reduce | flops 64 | bytes 512 | tf_op jit(solution)/shard_map/psum | solution.py:124
  72.2 1.3 collective-permute-start
  73.5 1.3 collective-permute-start.1
  74.8 1.6 fusion.139
  79.8 3.9 collective-permute-start.2
  85.6 10.1 %copy.82 = bf16[192,16384]{0,1:T(8,128)(2,1)} copy(bf16[192,16384]{1,0:T(8,128)(2,1)} %param.27) | data formatting | bytes 12582912 | tf_op args[11]
  95.7 6.2 %gather_fusion = bf16[512,192]{1,0:T(8,128)(2,1)S(1)} fusion(bf16[192,16384]{0,1:T(8,128)(2,1)} %copy.82, s32[1024]{0:T(1024)} %pad_clamp_fusion), kind=kCustom, calls=%fused_computation | custom fusion | bytes 395264 | tf_op jit(solution)/shard_map/jit(_take)/gather | solution.py:173
  104.9 1.7 collective-permute-start.7
  106.7 2.8 collective-permute-start.6
  109.5 13.9 %collective-permute-done.7 = bf16[192,3,1024]{2,0,1:T(8,128)(2,1)S(1)} collective-permute-done((bf16[192,3,1024]{2,0,1:T(8,128)(2,1)S(1)}, bf16[192,3,1024]{2,0,1:T(8,128)(2,1)S(1)}, u32[]{:S(2)}, u32[]{:S(2)}) %collective-permute-start.7) | collective-permute-done | bytes 1179680 | tf_op jit(solution)/shard_map/ppermute | solution.py:20
  123.4 11.1 %collective-permute-start.9 = (bf16[192,3,1024]{2,0,1:T(8,128)(2,1)S(1)}, bf16[192,3,1024]{2,0,1:T(8,128)(2,1)}, u32[]{:S(2)}, u32[]{:S(2)}) collective-permute-start(bf16[192,3,1024]{2,0,1:T(8,128)(2,1)S(1)} %collective-permute-done.7), channel_id=1, source_target_pairs={{0,2},{2,4},{4,6},{6,8},{8,10},{10,12},{12,14},{14,16},{16,18},{18... | collective-permute-start | bytes 3538952 | tf_op jit(solution)/shard_map/ppermute | solution.py:20
  135.5 6.4 %collective-permute-done.9 = bf16[192,3,1024]{2,0,1:T(8,128)(2,1)} collective-permute-done((bf16[192,3,1024]{2,0,1:T(8,128)(2,1)S(1)}, bf16[192,3,1024]{2,0,1:T(8,128)(2,1)}, u32[]{:S(2)}, u32[]{:S(2)}) %collective-permute-start.9) | collective-permute-done | bytes 1179680 | tf_op jit(solution)/shard_map/ppermute | solution.py:20
  141.9 19.7 %collective-permute-start.11 = (bf16[192,3,1024]{2,0,1:T(8,128)(2,1)}, bf16[192,3,1024]{2,0,1:T(8,128)(2,1)}, u32[]{:S(2)}, u32[]{:S(2)}) collective-permute-start(bf16[192,3,1024]{2,0,1:T(8,128)(2,1)} %collective-permute-done.9), channel_id=1, source_target_pairs={{0,2},{2,4},{4,6},{6,8},{8,10},{10,12},{12,14},{14,16},{16,18},{18... | collective-permute-start | bytes 3538952 | tf_op jit(solution)/shard_map/ppermute | solution.py:20
  162.5 1.3 fusion.140
  164.9 23.7 %collective-permute-start.13 = (bf16[192,3,1024]{2,0,1:T(8,128)(2,1)}, bf16[192,3,1024]{2,0,1:T(8,128)(2,1)S(1)}, u32[]{:S(2)}, u32[]{:S(2)}) collective-permute-start(bf16[192,3,1024]{2,0,1:T(8,128)(2,1)} %collective-permute-done.11), channel_id=1, source_target_pairs={{0,2},{2,4},{4,6},{6,8},{8,10},{10,12},{12,14},{14,16},{16,18},{18... | collective-permute-start | bytes 3538952 | tf_op jit(solution)/shard_map/ppermute | solution.py:20
  189.0 6.5 %all_gather.6 = bf16[32,3072]{1,0:T(8,128)(2,1)S(1)} all-gather(bf16[16,3072]{1,0:T(8,128)(2,1)S(1)} %add_convert_fusion.1), channel_id=1, replica_groups=mesh['seq'=16,'head'=2] {'head'}, dimensions={0}, use_global_device_ids=true | all-gather | bytes 294912 | tf_op jit(solution)/shard_map/all_gather | solution.py:159
  195.5 21.0 %collective-permute-start.15 = (bf16[192,3,1024]{2,0,1:T(8,128)(2,1)S(1)}, bf16[192,3,1024]{2,0,1:T(8,128)(2,1)S(1)}, u32[]{:S(2)}, u32[]{:S(2)}) collective-permute-start(bf16[192,3,1024]{2,0,1:T(8,128)(2,1)S(1)} %collective-permute-done.13), channel_id=1, source_target_pairs={{0,2},{2,4},{4,6},{6,8},{8,10},{10,12},{12,14},{14,16},{16,18},{18... | collective-permute-start | bytes 3538952 | tf_op jit(solution)/shard_map/ppermute | solution.py:20
  216.9 1.8 convolution_add_fusion.9
  220.4 5.2 %collective-permute-done.15 = bf16[192,3,1024]{2,0,1:T(8,128)(2,1)S(1)} collective-permute-done((bf16[192,3,1024]{2,0,1:T(8,128)(2,1)S(1)}, bf16[192,3,1024]{2,0,1:T(8,128)(2,1)S(1)}, u32[]{:S(2)}, u32[]{:S(2)}) %collective-permute-start.15) | collective-permute-done | bytes 1179680 | tf_op jit(solution)/shard_map/ppermute | solution.py:20
  225.6 19.1 %collective-permute-start.17 = (bf16[192,3,1024]{2,0,1:T(8,128)(2,1)S(1)}, bf16[192,3,1024]{2,0,1:T(8,128)(2,1)S(1)}, u32[]{:S(2)}, u32[]{:S(2)}) collective-permute-start(bf16[192,3,1024]{2,0,1:T(8,128)(2,1)S(1)} %collective-permute-done.15), channel_id=1, source_target_pairs={{0,2},{2,4},{4,6},{6,8},{8,10},{10,12},{12,14},{14,16},{16,18},{18... | collective-permute-start | bytes 3538952 | tf_op jit(solution)/shard_map/ppermute | solution.py:20
  244.7 1.6 fusion.95
  246.4 1.7 fusion.4
  248.0 1.6 fusion.92
  249.7 1.7 fusion.5
  251.8 21.2 %collective-permute-start.18 = (bf16[192,3,1024]{2,0,1:T(8,128)(2,1)S(1)}, bf16[192,3,1024]{2,0,1:T(8,128)(2,1)S(1)}, u32[]{:S(2)}, u32[]{:S(2)}) collective-permute-start(bf16[192,3,1024]{2,0,1:T(8,128)(2,1)S(1)} %collective-permute-done.17), channel_id=1, source_target_pairs={{0,2},{2,4},{4,6},{6,8},{8,10},{10,12},{12,14},{14,16},{16,18},{18... | collective-permute-start | bytes 3538952 | tf_op jit(solution)/shard_map/ppermute | solution.py:20
  278.0 42.6 %all-reduce.1 = (f32[512]{0:T(512)S(1)}, f32[512]{0:T(512)S(1)}) all-reduce(f32[512]{0:T(512)S(1)} %get-tuple-element.16, f32[512]{0:T(512)S(1)} %get-tuple-element.15), channel_id=1, replica_groups=mesh['seq'=16,'head'=2] {'seq'}, use_global_device_ids=true, to_apply=%region_9.10 | all-reduce | flops 1024 | bytes 8192 | tf_op jit(solution)/shard_map/psum | solution.py:177
  320.6 3.9 fusion.19
  324.5 94.8 %all-reduce.3 = bf16[512,2,1024]{2,0,1:T(8,128)(2,1)S(1)} all-reduce(f32[512,2,1024]{2,0,1:T(8,128)} %fusion.19), channel_id=1, replica_groups=mesh['seq'=16,'head'=2] {'seq'}, use_global_device_ids=true, to_apply=%region_10.11 | all-reduce | flops 1048576 | bytes 6291456 | tf_op jit(solution)/shard_map/psum | solution.py:186
  422.2 2.4 copy.103
  426.5 2.0 fusion.49
  428.5 16.9 %reduce-scatter.2.cloned.1.call-done = f32[16,3072]{1,0:T(8,128)} async-done(((f32[32,3072]{1,0:T(8,128)}), f32[16,3072]{1,0:T(8,128)}) %reduce-scatter.2.cloned.1.call-update) | async-done | bytes 196624 | tf_op jit(solution)/shard_map/reduce_scatter | solution.py:202
  (164 shorter events, 27.2 us)
Async XLA Ops:
  6.5 314.1 %copy-start = (bf16[192,2,1024]{2,1,0:T(2,128)(2,1)S(1)}, bf16[192,2,1024]{2,1,0:T(2,128)(2,1)}, u32[]{:S(2)}) copy-start(bf16[192,2,1024]{2,1,0:T(2,128)(2,1)} %param.29) | copy-start | bytes 2359300
  6.5 415.6 %all-gather.2.cloned.1.call-start = ((), (), s32[]{:S(2)}) async-start(), calls=%async_computation.1 | async-start | bytes 2228224 | tf_op jit(solution)/shard_map/all_gather | solution.py:196
  6.5 100.1 %collective-permute-start.4 = (bf16[192,3,1024]{2,0,1:T(8,128)(2,1)}, bf16[192,3,1024]{2,0,1:T(8,128)(2,1)S(1)}, u32[]{:S(2)}, u32[]{:S(2)}) collective-permute-start(bf16[192,3,1024]{2,0,1:T(8,128)(2,1)} %param.24), channel_id=1, source_target_pairs={{0,30},{2,0},{4,2},{6,4},{8,6},{10,8},{12,10},{14,12},{16,14},{18,... | collective-permute-start | bytes 3538952 | tf_op jit(solution)/shard_map/ppermute | solution.py:22
  13.2 91.6 %collective-permute-start.5 = (bf16[192,3,1024]{2,0,1:T(8,128)(2,1)}, bf16[192,3,1024]{2,0,1:T(8,128)(2,1)S(1)}, u32[]{:S(2)}, u32[]{:S(2)}) collective-permute-start(bf16[192,3,1024]{2,0,1:T(8,128)(2,1)} %param.24), channel_id=1, source_target_pairs={{0,2},{2,4},{4,6},{6,8},{8,10},{10,12},{12,14},{14,16},{16,18},{18... | collective-permute-start | bytes 3538952 | tf_op jit(solution)/shard_map/ppermute | solution.py:20
  72.2 6.1 %collective-permute-start = (bf16[8,1,4,512]{3,0,2,1:T(8,128)(2,1)S(1)}, bf16[8,1,4,512]{3,0,2,1:T(8,128)(2,1)S(1)}, u32[]{:S(2)}, u32[]{:S(2)}) collective-permute-start(bf16[8,1,4,512]{3,0,2,1:T(8,128)(2,1)S(1)} %get-tuple-element.41), channel_id=1, source_target_pairs={{0,2},{2,4},{4,6},{6,8},{8,10},{10,12},{12,14},{14,16},{16,18},{18... | collective-permute-start | bytes 98312 | tf_op jit(solution)/shard_map/ppermute | solution.py:36
  73.5 5.6 %collective-permute-start.1 = (bf16[8,1,4,512]{3,0,2,1:T(8,128)(2,1)S(1)}, bf16[8,1,4,512]{3,0,2,1:T(8,128)(2,1)S(1)}, u32[]{:S(2)}, u32[]{:S(2)}) collective-permute-start(bf16[8,1,4,512]{3,0,2,1:T(8,128)(2,1)S(1)} %get-tuple-element.42), channel_id=1, source_target_pairs={{2,0},{4,2},{6,4},{8,6},{10,8},{12,10},{14,12},{16,14},{18,16},{20... | collective-permute-start | bytes 98312 | tf_op jit(solution)/shard_map/ppermute | solution.py:38
  79.8 22.1 %collective-permute-start.2 = (bf16[8,4,1,512]{3,0,2,1:T(8,128)(2,1)}, bf16[8,4,1,512]{3,0,2,1:T(8,128)(2,1)}, u32[]{:S(2)}, u32[]{:S(2)}) collective-permute-start(bf16[8,4,1,512]{3,0,2,1:T(8,128)(2,1)} %get-tuple-element.39), channel_id=1, source_target_pairs={{0,1},{2,3},{4,5},{6,7},{8,9},{10,11},{12,13},{14,15},{16,17},{18,... | collective-permute-start | bytes 98312 | tf_op jit(solution)/shard_map/ppermute | solution.py:36
  83.7 18.2 %collective-permute-start.3 = (bf16[8,4,1,512]{3,0,2,1:T(8,128)(2,1)}, bf16[8,4,1,512]{3,0,2,1:T(8,128)(2,1)}, u32[]{:S(2)}, u32[]{:S(2)}) collective-permute-start(bf16[8,4,1,512]{3,0,2,1:T(8,128)(2,1)} %get-tuple-element.40), channel_id=1, source_target_pairs={{1,0},{3,2},{5,4},{7,6},{9,8},{11,10},{13,12},{15,14},{17,16},{19,... | collective-permute-start | bytes 98312 | tf_op jit(solution)/shard_map/ppermute | solution.py:38
  103.7 31.7 %copy-start.11 = (bf16[8,2,4,512]{3,2,1,0:T(4,128)(2,1)S(1)}, bf16[8,2,4,512]{3,2,1,0:T(4,128)(2,1)}, u32[]{:S(2)}) copy-start(bf16[8,2,4,512]{3,2,1,0:T(4,128)(2,1)} %param.16) | copy-start | bytes 196612
  103.7 31.7 %copy-start.16 = (f32[512]{0:T(512)S(1)}, f32[512]{0:T(512)}, u32[]{:S(2)}) copy-start(f32[512]{0:T(512)} %copy-done.15) | copy-start | bytes 6148
  103.8 31.7 %copy-start.18 = (f32[512]{0:T(512)S(1)}, f32[512]{0:T(512)}, u32[]{:S(2)}) copy-start(f32[512]{0:T(512)} %param.18) | copy-start | bytes 6148
  103.8 57.9 %copy-start.12 = (bf16[3,3,3,16,512]{4,3,2,1,0:T(8,128)(2,1)S(1)}, bf16[3,3,3,16,512]{4,3,2,1,0:T(8,128)(2,1)}, u32[]{:S(2)}) copy-start(bf16[3,3,3,16,512]{4,3,2,1,0:T(8,128)(2,1)} %param.19) | copy-start | bytes 1327108
  103.9 57.9 %copy-start.21 = (f32[16]{0:T(128)S(1)}, f32[16]{0:T(128)}, u32[]{:S(2)}) copy-start(f32[16]{0:T(128)} %param.20) | copy-start | bytes 196
  104.9 56.9 %copy-start.4 = (bf16[192,3,1024]{2,0,1:T(8,128)(2,1)}, bf16[192,3,1024]{2,0,1:T(8,128)(2,1)S(1)}, u32[]{:S(2)}) copy-start(bf16[192,3,1024]{2,0,1:T(8,128)(2,1)S(1)} %collective-permute-done.5) | copy-start | bytes 3538948
  104.9 18.5 %collective-permute-start.7 = (bf16[192,3,1024]{2,0,1:T(8,128)(2,1)S(1)}, bf16[192,3,1024]{2,0,1:T(8,128)(2,1)S(1)}, u32[]{:S(2)}, u32[]{:S(2)}) collective-permute-start(bf16[192,3,1024]{2,0,1:T(8,128)(2,1)S(1)} %collective-permute-done.5), channel_id=1, source_target_pairs={{0,2},{2,4},{4,6},{6,8},{8,10},{10,12},{12,14},{14,16},{16,18},{18... | collective-permute-start | bytes 3538952 | tf_op jit(solution)/shard_map/ppermute | solution.py:20
  106.7 55.1 %copy-start.3 = (bf16[192,3,1024]{2,0,1:T(8,128)(2,1)}, bf16[192,3,1024]{2,0,1:T(8,128)(2,1)S(1)}, u32[]{:S(2)}) copy-start(bf16[192,3,1024]{2,0,1:T(8,128)(2,1)S(1)} %collective-permute-done.4) | copy-start | bytes 3538948
  106.7 28.6 %collective-permute-start.6 = (bf16[192,3,1024]{2,0,1:T(8,128)(2,1)S(1)}, bf16[192,3,1024]{2,0,1:T(8,128)(2,1)S(1)}, u32[]{:S(2)}, u32[]{:S(2)}) collective-permute-start(bf16[192,3,1024]{2,0,1:T(8,128)(2,1)S(1)} %collective-permute-done.4), channel_id=1, source_target_pairs={{0,30},{2,0},{4,2},{6,4},{8,6},{10,8},{12,10},{14,12},{16,14},{18,... | collective-permute-start | bytes 3538952 | tf_op jit(solution)/shard_map/ppermute | solution.py:22
  123.4 38.4 %copy-start.6 = (bf16[192,3,1024]{2,0,1:T(8,128)(2,1)}, bf16[192,3,1024]{2,0,1:T(8,128)(2,1)S(1)}, u32[]{:S(2)}) copy-start(bf16[192,3,1024]{2,0,1:T(8,128)(2,1)S(1)} %collective-permute-done.7) | copy-start | bytes 3538948
  123.4 18.5 %collective-permute-start.9 = (bf16[192,3,1024]{2,0,1:T(8,128)(2,1)S(1)}, bf16[192,3,1024]{2,0,1:T(8,128)(2,1)}, u32[]{:S(2)}, u32[]{:S(2)}) collective-permute-start(bf16[192,3,1024]{2,0,1:T(8,128)(2,1)S(1)} %collective-permute-done.7), channel_id=1, source_target_pairs={{0,2},{2,4},{4,6},{6,8},{8,10},{10,12},{12,14},{14,16},{16,18},{18... | collective-permute-start | bytes 3538952 | tf_op jit(solution)/shard_map/ppermute | solution.py:20
  135.3 26.4 %collective-permute-start.8 = (bf16[192,3,1024]{2,0,1:T(8,128)(2,1)S(1)}, bf16[192,3,1024]{2,0,1:T(8,128)(2,1)}, u32[]{:S(2)}, u32[]{:S(2)}) collective-permute-start(bf16[192,3,1024]{2,0,1:T(8,128)(2,1)S(1)} %collective-permute-done.6), channel_id=1, source_target_pairs={{0,30},{2,0},{4,2},{6,4},{8,6},{10,8},{12,10},{14,12},{16,14},{18,... | collective-permute-start | bytes 3538952 | tf_op jit(solution)/shard_map/ppermute | solution.py:22
  141.9 23.0 %collective-permute-start.11 = (bf16[192,3,1024]{2,0,1:T(8,128)(2,1)}, bf16[192,3,1024]{2,0,1:T(8,128)(2,1)}, u32[]{:S(2)}, u32[]{:S(2)}) collective-permute-start(bf16[192,3,1024]{2,0,1:T(8,128)(2,1)} %collective-permute-done.9), channel_id=1, source_target_pairs={{0,2},{2,4},{4,6},{6,8},{8,10},{10,12},{12,14},{14,16},{16,18},{18... | collective-permute-start | bytes 3538952 | tf_op jit(solution)/shard_map/ppermute | solution.py:20
  161.7 27.2 %collective-permute-start.10 = (bf16[192,3,1024]{2,0,1:T(8,128)(2,1)}, bf16[192,3,1024]{2,0,1:T(8,128)(2,1)}, u32[]{:S(2)}, u32[]{:S(2)}) collective-permute-start(bf16[192,3,1024]{2,0,1:T(8,128)(2,1)} %collective-permute-done.8), channel_id=1, source_target_pairs={{0,30},{2,0},{4,2},{6,4},{8,6},{10,8},{12,10},{14,12},{16,14},{18,... | collective-permute-start | bytes 3538952 | tf_op jit(solution)/shard_map/ppermute | solution.py:22
  161.8 54.8 %copy-start.2 = (bf16[192,3,1024]{2,0,1:T(8,128)(2,1)S(1)}, bf16[192,3,1024]{2,0,1:T(8,128)(2,1)}, u32[]{:S(2)}) copy-start(bf16[192,3,1024]{2,0,1:T(8,128)(2,1)} %param.24) | copy-start | bytes 3538948
  164.9 30.6 %collective-permute-start.13 = (bf16[192,3,1024]{2,0,1:T(8,128)(2,1)}, bf16[192,3,1024]{2,0,1:T(8,128)(2,1)S(1)}, u32[]{:S(2)}, u32[]{:S(2)}) collective-permute-start(bf16[192,3,1024]{2,0,1:T(8,128)(2,1)} %collective-permute-done.11), channel_id=1, source_target_pairs={{0,2},{2,4},{4,6},{6,8},{8,10},{10,12},{12,14},{14,16},{16,18},{18... | collective-permute-start | bytes 3538952 | tf_op jit(solution)/shard_map/ppermute | solution.py:20
  188.8 30.7 %collective-permute-start.12 = (bf16[192,3,1024]{2,0,1:T(8,128)(2,1)}, bf16[192,3,1024]{2,0,1:T(8,128)(2,1)S(1)}, u32[]{:S(2)}, u32[]{:S(2)}) collective-permute-start(bf16[192,3,1024]{2,0,1:T(8,128)(2,1)} %collective-permute-done.10), channel_id=1, source_target_pairs={{0,30},{2,0},{4,2},{6,4},{8,6},{10,8},{12,10},{14,12},{16,14},{18,... | collective-permute-start | bytes 3538952 | tf_op jit(solution)/shard_map/ppermute | solution.py:22
  195.5 30.1 %collective-permute-start.15 = (bf16[192,3,1024]{2,0,1:T(8,128)(2,1)S(1)}, bf16[192,3,1024]{2,0,1:T(8,128)(2,1)S(1)}, u32[]{:S(2)}, u32[]{:S(2)}) collective-permute-start(bf16[192,3,1024]{2,0,1:T(8,128)(2,1)S(1)} %collective-permute-done.13), channel_id=1, source_target_pairs={{0,2},{2,4},{4,6},{6,8},{8,10},{10,12},{12,14},{14,16},{16,18},{18... | collective-permute-start | bytes 3538952 | tf_op jit(solution)/shard_map/ppermute | solution.py:20
  219.5 31.9 %collective-permute-start.14 = (bf16[192,3,1024]{2,0,1:T(8,128)(2,1)S(1)}, bf16[192,3,1024]{2,0,1:T(8,128)(2,1)S(1)}, u32[]{:S(2)}, u32[]{:S(2)}) collective-permute-start(bf16[192,3,1024]{2,0,1:T(8,128)(2,1)S(1)} %collective-permute-done.12), channel_id=1, source_target_pairs={{0,30},{2,0},{4,2},{6,4},{8,6},{10,8},{12,10},{14,12},{16,14},{18,... | collective-permute-start | bytes 3538952 | tf_op jit(solution)/shard_map/ppermute | solution.py:22
  225.6 26.2 %collective-permute-start.17 = (bf16[192,3,1024]{2,0,1:T(8,128)(2,1)S(1)}, bf16[192,3,1024]{2,0,1:T(8,128)(2,1)S(1)}, u32[]{:S(2)}, u32[]{:S(2)}) collective-permute-start(bf16[192,3,1024]{2,0,1:T(8,128)(2,1)S(1)} %collective-permute-done.15), channel_id=1, source_target_pairs={{0,2},{2,4},{4,6},{6,8},{8,10},{10,12},{12,14},{14,16},{16,18},{18... | collective-permute-start | bytes 3538952 | tf_op jit(solution)/shard_map/ppermute | solution.py:20
  251.4 23.2 %collective-permute-start.16 = (bf16[192,3,1024]{2,0,1:T(8,128)(2,1)S(1)}, bf16[192,3,1024]{2,0,1:T(8,128)(2,1)S(1)}, u32[]{:S(2)}, u32[]{:S(2)}) collective-permute-start(bf16[192,3,1024]{2,0,1:T(8,128)(2,1)S(1)} %collective-permute-done.14), channel_id=1, source_target_pairs={{0,30},{2,0},{4,2},{6,4},{8,6},{10,8},{12,10},{14,12},{16,14},{18,... | collective-permute-start | bytes 3538952 | tf_op jit(solution)/shard_map/ppermute | solution.py:22
  251.8 24.0 %collective-permute-start.18 = (bf16[192,3,1024]{2,0,1:T(8,128)(2,1)S(1)}, bf16[192,3,1024]{2,0,1:T(8,128)(2,1)S(1)}, u32[]{:S(2)}, u32[]{:S(2)}) collective-permute-start(bf16[192,3,1024]{2,0,1:T(8,128)(2,1)S(1)} %collective-permute-done.17), channel_id=1, source_target_pairs={{0,2},{2,4},{4,6},{6,8},{8,10},{10,12},{12,14},{14,16},{16,18},{18... | collective-permute-start | bytes 3538952 | tf_op jit(solution)/shard_map/ppermute | solution.py:20
  275.0 45.7 %copy-start.22 = (f32[2,192]{1,0:T(2,128)S(1)}, f32[2,192]{1,0:T(2,128)}, u32[]{:S(2)}) copy-start(f32[2,192]{1,0:T(2,128)} %param.28) | copy-start | bytes 4612
  277.6 167.8 %reduce-scatter.2.cloned.1.call-start = ((), (), s32[]{:S(2)}) async-start(), calls=%async_computation.2 | async-start | bytes 589824 | tf_op jit(solution)/shard_map/reduce_scatter | solution.py:202
  (14 other events, 182.6 us)
Sparse Core Ops, SparseCore 0:
  277.7 59.3 all-gather.1
  428.6 16.6 reduce-scatter.1
